TPU v7x, 128 devices: a whole 4x4x4 slice. The times are simulated.
128 devices in a mesh: leaf: 4 (over y_hi, core), front: 32 (over y_lo, z, x).
Axes of the slice: x: 4, y: 4 (y_hi: 2, y_lo: 2; y = y_hi * 2 + y_lo), z: 4, core: 2. Of those that a mesh axis runs over, the one named last changes fastest.
Arguments:
- leaf_source: float32 [4, 2048, 128], P('leaf', 'front'), may hold values from -6 to 6
- mid_source: float32 [4, 2048, 128], P('leaf', 'front'), may hold values from -6 to 6
- root_source: float32 [8192, 128], P('front'), may hold values from -6 to 6
- leaf_inverse: float32 [4, 2, 2048, 2048], P('leaf', None, 'front'), may hold values from -0.09375 to 0.09375
- leaf_coupling: float32 [4, 2, 4096, 2048], P('leaf', None, None, 'front'), may hold values from -0.09375 to 0.09375
- mid_inverse: float32 [4, 2, 2048, 4096], P('leaf', None, None, 'front'), may hold values from -0.0625 to 0.0625
- mid_coupling: float32 [4, 2, 8192, 2048], P('leaf', None, None, 'front'), may hold values from -0.0625 to 0.0625
- root_inverse: float32 [2, 8192, 8192], P(None, 'leaf', 'front'), may hold values from -0.046875 to 0.046875
- leaf_blocks: int32 [4, 32], P('leaf'), may hold values from 0 to 31, as said below
- mid_blocks: int32 [2, 64], replicated, may hold values from 0 to 63, as said below
Outputs:
- leaf_solution: float32 [4, 2048, 128], P('leaf', 'front')
- mid_solution: float32 [4, 2048, 128], P('leaf', 'front')
- root_solution: float32 [8192, 128], P('front')
Inputs may be any that keep to these rules, and one draw needn't show every extreme that they name: `leaf_blocks`: each row holds every block number of a level-1 separator exactly once. `mid_blocks`: each row holds every block number of the root separator exactly once.
All inputs are finite; a program needn't handle non-finite values.
Results may differ from a plain program's by a relative error of at most 0.00015.
Values sent between devices are 32-bit elements; how exact they have to be, the bound alone decides.
A program may use at most 128 MiB of HBM per device.

v0:
```python
import jax
import jax.numpy as jnp
from jax import lax
from jax.sharding import PartitionSpec as P

exact_precision = lax.Precision.HIGHEST


def partner(value, axis, apart):
    return lax.ppermute(value, axis, [(i, i ^ 1 << apart) for i in range(lax.axis_size(axis))])


def complex_apply(matrix, vectors):
    width = vectors.shape[1] // 2
    real_part = jnp.dot(
        matrix[0], vectors, precision=exact_precision, preferred_element_type=jnp.float32
    )
    imag_part = jnp.dot(
        matrix[1], vectors, precision=exact_precision, preferred_element_type=jnp.float32
    )
    return jnp.concatenate(
        [real_part[:, :width] - imag_part[:, width:], real_part[:, width:] + imag_part[:, :width]],
        axis=1,
    )


def complex_transposed(matrix, vectors):
    width = vectors.shape[1] // 2
    dims = (((0,), (0,)), ((), ()))
    real_part = lax.dot_general(
        matrix[0], vectors, dims, precision=exact_precision, preferred_element_type=jnp.float32
    )
    imag_part = lax.dot_general(
        matrix[1], vectors, dims, precision=exact_precision, preferred_element_type=jnp.float32
    )
    return jnp.concatenate(
        [real_part[:, :width] - imag_part[:, width:], real_part[:, width:] + imag_part[:, :width]],
        axis=1,
    )


def pick_rows(matrix, block_order, row_count):
    positions = jnp.arange(row_count, dtype=jnp.int32)
    sources = jnp.take(block_order, positions // 128) * 128 + positions % 128
    return jnp.take(matrix, sources, axis=1)


def gather_rows(local_rows, update, initial):
    return update(initial, lax.all_gather(local_rows, "front", axis=0, tiled=True), jnp.int32(0))


def scatter_rows(term, rows_each):
    return lax.psum_scatter(
        term(jnp.int32(0), rows_each * lax.axis_size("front")),
        "front",
        scatter_dimension=0,
        tiled=True,
    )


def pair_swap(values):
    return partner(values, "leaf", 0)


def group_total(values):
    return lax.psum(values, "leaf")


def body(
    leaf_source,
    mid_source,
    root_source,
    leaf_inverse,
    leaf_coupling,
    mid_inverse,
    mid_coupling,
    root_inverse,
    leaf_blocks,
    mid_blocks,
):
    front_count = lax.axis_size("front")
    group = lax.axis_index("leaf")
    side = group % 2
    source_two = leaf_source[0]
    inverse_two = leaf_inverse[0]
    coupling_two = leaf_coupling[0]
    inverse_one = mid_inverse[0]
    coupling_one = mid_coupling[0]
    order_two = jnp.argsort(leaf_blocks[0])
    order_one = jnp.argsort(lax.dynamic_index_in_dim(mid_blocks, group // 2, 0, keepdims=False))
    width2 = source_two.shape[1]
    rows_two = source_two.shape[0]
    half_rows = mid_source.shape[1]
    block_rows = coupling_two.shape[1] // front_count
    root_block = root_source.shape[0]

    def fold_inverse_two(carry, shard_piece, row_start):
        return complex_apply(inverse_two, shard_piece)

    solved_two = gather_rows(source_two, fold_inverse_two, jnp.zeros(source_two.shape, jnp.float32))

    def lift_two(row_start, row_count):
        return complex_apply(pick_rows(coupling_two, order_two, row_count), solved_two)

    lifted = scatter_rows(lift_two, block_rows)
    placed = lax.dynamic_update_slice_in_dim(
        jnp.zeros((block_rows, width2), jnp.float32), mid_source[0], side * half_rows, 0
    )
    own_part = placed - lifted
    reduced_one = own_part + pair_swap(own_part)

    def apply_one(row_start, row_count):
        return complex_apply(inverse_one, reduced_one)

    solved_one = scatter_rows(apply_one, half_rows)

    def lift_one(row_start, row_count):
        return complex_apply(pick_rows(coupling_one, order_one, row_count), solved_one)

    gathered_terms = group_total(scatter_rows(lift_one, root_block))
    reduced_root = root_source - gathered_terms

    def apply_root(row_start, row_count):
        return complex_apply(root_inverse, reduced_root)

    solved_root = scatter_rows(apply_root, root_inverse.shape[1] // front_count)

    def fold_root(carry, shard_piece, row_start):
        return complex_transposed(root_inverse, shard_piece)

    partial_root = gather_rows(solved_root, fold_root, jnp.zeros(root_source.shape, jnp.float32))
    root_solution = group_total(partial_root)

    def fold_mid(carry, shard_piece, row_start):
        return complex_transposed(
            pick_rows(coupling_one, order_one, shard_piece.shape[0]), shard_piece
        )

    pulled_one = gather_rows(root_solution, fold_mid, jnp.zeros(solved_one.shape, jnp.float32))
    rest_one = solved_one - pulled_one

    def fold_inverse_one(carry, shard_piece, row_start):
        return complex_transposed(inverse_one, shard_piece)

    own_columns = gather_rows(
        rest_one, fold_inverse_one, jnp.zeros((block_rows, width2), jnp.float32)
    )
    mid_block = own_columns + pair_swap(own_columns)
    mid_solution = lax.dynamic_slice_in_dim(mid_block, side * half_rows, half_rows, 0)

    def fold_leaf(carry, shard_piece, row_start):
        return complex_transposed(
            pick_rows(coupling_two, order_two, shard_piece.shape[0]), shard_piece
        )

    pulled_two = gather_rows(mid_block, fold_leaf, jnp.zeros(solved_two.shape, jnp.float32))
    rest_two = solved_two - pulled_two

    def apply_leaf_back(row_start, row_count):
        return complex_transposed(inverse_two, rest_two)

    leaf_solution = scatter_rows(apply_leaf_back, rows_two)
    return (leaf_solution[None], mid_solution[None], root_solution)


def solution(mesh):
    placed = (
        P("leaf", "front", None),
        P("leaf", "front", None),
        P("front", None),
        P("leaf", None, "front", None),
        P("leaf", None, None, "front"),
        P("leaf", None, None, "front"),
        P("leaf", None, None, "front"),
        P(None, "leaf", "front"),
        P("leaf", None),
        P(),
    )
    return jax.shard_map(
        body,
        mesh=mesh,
        in_specs=placed,
        out_specs=(P("leaf", "front", None), P("leaf", "front", None), P("front", None)),
        check_vma=False,
    )
```

profile of v0, /device:TPU:0, one launch (start us, length us, event | category | flops | bytes accessed | tf_op | source)
XLA Modules:
  0.0 1807.4 jit_solution(7411422771738973150)
XLA Ops:
  8.0 2.3 sort.34
  11.7 6.2 copy.32
  17.8 19.9 %broadcast_clamp_fusion.1 = s32[4096]{0:T(1024)S(1)} fusion(s32[]{:T(128)} %bitcast.35, s32[]{:T(128)} %bitcast.34, s32[]{:T(128)} %bitcast.33, s32[]{:T(128)} %bitcast.32, s32[]{:T(128)} %bitcast.31, s32[]{:T(128)} %bitcast.30, s32[]{:T(128)} %bitcast.29, s32[]{:T(128)} %bitcast.28, s32[]{:T(128)} %bitcast.27, s32[]{:T(128)} %bitcast.26, s32[]{:T(128)} %bitcast.25, ...), kind=kLoop, calls=%fused_computation.211 | loop fusion | flops 356352 | bytes 16512 | tf_op gather
  37.7 30.5 %gather_fusion = f32[4096,2,64]{2,1,0:T(2,128)} fusion(f32[2,4096,64]{2,0,1:T(2,128)} %bitcast.203, s32[4096]{0:T(1024)S(1)} %broadcast_clamp_fusion.1), kind=kCustom, calls=%fused_computation.clone | custom fusion | bytes 4210688 | tf_op jit(solution)/shard_map/jit(_take)/gather | solution.py:45
  68.3 19.9 %compare_and_fusion.1 = pred[4096]{0:T(1024)(128)(4,1)S(1)} fusion(s32[]{:T(128)} %bitcast.35, s32[]{:T(128)} %bitcast.34, s32[]{:T(128)} %bitcast.33, s32[]{:T(128)} %bitcast.32, s32[]{:T(128)} %bitcast.31, s32[]{:T(128)} %bitcast.30, s32[]{:T(128)} %bitcast.29, s32[]{:T(128)} %bitcast.28, s32[]{:T(128)} %bitcast.27, s32[]{:T(128)} %bitcast.26, ...), kind=kLoop, calls=%fused_computation.210 | loop fusion | flops 364544 | bytes 4224 | tf_op jit(solution)/shard_map/jit(_take)/and | solution.py:45
  88.2 16.3 select_bitcast_fusion.1
  104.5 4.1 fusion.158
  108.6 54.6 %all-gather.15.cloned.1.call-done = f32[1,2048,128]{2,1,0:T(8,128)} async-done(((f32[1,64,128]{2,1,0:T(8,128)}), f32[1,2048,128]{2,1,0:T(8,128)}) %all-gather.15.cloned.1.call-update) | async-done | bytes 1048592 | tf_op jit(solution)/shard_map/all_gather | solution.py:49
  163.2 2.1 fusion.20
  165.4 2.0 fusion.22
  167.5 2.1 fusion.165
  169.6 2.1 fusion.166
  172.1 1.5 pad_maximum_fusion.1
  173.8 2.0 sort.35
  179.1 39.6 %compare_and_fusion = (pred[8192]{0:T(1024)(128)(4,1)S(1)}, s32[8192]{0:T(1024)S(1)}) fusion(s32[]{:T(128)} %bitcast.109, s32[]{:T(128)} %bitcast.108, s32[]{:T(128)} %bitcast.107, s32[]{:T(128)} %bitcast.106, s32[]{:T(128)} %bitcast.105, s32[]{:T(128)} %bitcast.104, s32[]{:T(128)} %bitcast.103, s32[]{:T(128)} %bitcast.102, s32[]{:T(128)} %bitcast.101, ...), kind=kLoop, calls=%fused_computation.166 | loop fusion | flops 1253376 | bytes 41216 | tf_op jit(solution)/shard_map/jit(_take)/and | solution.py:45
  218.7 118.7 %reduce-scatter.12.cloned.1.call-done = f32[128,128]{0,1:T(8,128)} async-done(((f32[4096,128]{0,1:T(8,128)}), f32[128,128]{0,1:T(8,128)}) %reduce-scatter.12.cloned.1.call-update) | async-done | bytes 65552 | tf_op jit(solution)/shard_map/reduce_scatter | solution.py:53
  338.5 10.8 copy.34
  349.3 59.6 %gather_fusion.1 = f32[8192,2,64]{2,1,0:T(2,128)} fusion(f32[2,8192,64]{2,0,1:T(2,128)} %bitcast.198, s32[8192]{0:T(1024)S(1)} %broadcast_clamp_fusion), kind=kCustom, calls=%fused_computation.1.clone | custom fusion | bytes 8421376 | tf_op jit(solution)/shard_map/jit(_take)/gather | solution.py:45
  408.9 2.2 convolution_bitcast_fusion.3
  411.1 2.2 convolution_bitcast_fusion.2
  414.6 2.6 copy.41
  417.3 29.5 %select_bitcast_fusion = f32[2,8192,64]{2,0,1:T(2,128)S(1)} fusion(f32[8192,2,64]{2,1,0:T(2,128)} %gather_fusion.1, pred[8192]{0:T(1024)(128)(4,1)S(1)} %get-tuple-element.20), kind=kLoop, calls=%fused_computation.2 | loop fusion | flops 1048576 | bytes 8396800 | tf_op jit(solution)/shard_map/jit(_take)/select_n | solution.py:45
  446.8 7.7 fusion.157
  454.5 120.2 %reduce-scatter.16.cloned.1.call-done = f32[64,128]{1,0:T(8,128)} async-done(((f32[2048,128]{1,0:T(8,128)}), f32[64,128]{1,0:T(8,128)}) %reduce-scatter.16.cloned.1.call-update) | async-done | bytes 32784
  574.7 6.0 fusion.167
  580.8 4.4 fusion.168
  585.7 2.3 pad_maximum_fusion
  588.1 165.2 %reduce-scatter.14.cloned.1.call-done = f32[256,128]{0,1:T(8,128)} async-done(((f32[8192,128]{0,1:T(8,128)}), f32[256,128]{0,1:T(8,128)}) %reduce-scatter.14.cloned.1.call-update) | async-done | bytes 131088 | tf_op jit(solution)/shard_map/reduce_scatter | solution.py:53
  753.9 38.4 %all-reduce.3.cloned.1.call-done = f32[256,128]{0,1:T(8,128)} async-done(((f32[256,128]{0,1:T(8,128)}), f32[256,128]{0,1:T(8,128)}) %all-reduce.3.cloned.1.call-update) | async-done | bytes 131088 | tf_op jit(solution)/shard_map/psum | solution.py:66
  792.3 3.9 convolution_bitcast_fusion.5
  796.2 3.9 convolution_bitcast_fusion.4
  801.3 2.6 copy.43
  803.9 160.8 %reduce-scatter.18.cloned.1.call-done = f32[64,128]{1,0:T(8,128)} async-done(((f32[2048,128]{1,0:T(8,128)}), f32[64,128]{1,0:T(8,128)}) %reduce-scatter.18.cloned.1.call-update) | async-done | bytes 32784 | tf_op jit(solution)/shard_map/reduce_scatter | solution.py:53
  964.8 148.6 %all-gather.7.cloned.1.call-done = f32[2048,128]{1,0:T(8,128)} async-done(((f32[64,128]{1,0:T(8,128)}), f32[2048,128]{1,0:T(8,128)}) %all-gather.7.cloned.1.call-update) | async-done | bytes 1048592 | tf_op jit(solution)/shard_map/all_gather | solution.py:49
  1113.4 3.8 fusion.10
  1117.2 3.8 fusion.13
  1121.7 40.5 %all-reduce.5.cloned.1.call-done = f32[256,128]{0,1:T(8,128)} async-done(((f32[256,128]{0,1:T(8,128)}), f32[256,128]{0,1:T(8,128)}) %all-reduce.5.cloned.1.call-update) | async-done | bytes 131088 | tf_op jit(solution)/shard_map/psum | solution.py:66
  1162.4 158.7 %all-gather.9.cloned.1.call-done = f32[8192,128]{0,1:T(8,128)} async-done(((f32[256,128]{0,1:T(8,128)}), f32[8192,128]{0,1:T(8,128)}) %all-gather.9.cloned.1.call-update) | async-done | bytes 4194320 | tf_op jit(solution)/shard_map/all_gather | solution.py:49
  1321.1 10.3 fusion.169
  1331.5 7.1 fusion.170
  1339.4 150.8 %all-gather.11.cloned.1.call-done = f32[2048,128]{1,0:T(8,128)} async-done(((f32[64,128]{1,0:T(8,128)}), f32[2048,128]{1,0:T(8,128)}) %all-gather.11.cloned.1.call-update) | async-done | bytes 1048592 | tf_op jit(solution)/shard_map/all_gather | solution.py:49
  1490.3 3.4 convolution_bitcast_fusion.6
  1493.6 3.4 convolution_bitcast_fusion.7
  1499.0 125.6 %all-gather.13.cloned.1.call-done = f32[4096,128]{0,1:T(8,128)} async-done(((f32[128,128]{0,1:T(8,128)}), f32[4096,128]{0,1:T(8,128)}) %all-gather.13.cloned.1.call-update) | async-done | bytes 2097168 | tf_op jit(solution)/shard_map/all_gather | solution.py:49
  1624.6 5.8 fusion.171
  1630.5 3.5 fusion.172
  1636.6 1.3 copy.45
  1639.5 159.1 %reduce-scatter.20.cloned.1.call-done = f32[64,128]{1,0:T(8,128)} async-done(((f32[2048,128]{1,0:T(8,128)}), f32[64,128]{1,0:T(8,128)}) %reduce-scatter.20.cloned.1.call-update) | async-done | bytes 32784
  (94 shorter events, 20.3 us)
Async XLA Ops:
  7.2 166.6 %copy-start = (s32[2,64]{1,0:T(2,128)S(1)}, s32[2,64]{1,0:T(2,128)}, u32[]{:S(2)}) copy-start(s32[2,64]{1,0:T(2,128)} %param.27) | copy-start | bytes 1540
  7.2 156.1 %all-gather.15.cloned.1.call-start = ((), (), s32[]{:S(2)}) async-start(), calls=%async_computation.13 | async-start | bytes 1081344 | tf_op jit(solution)/shard_map/all_gather | solution.py:49
  7.9 329.5 %reduce-scatter.12.cloned.1.call-start = ((), (), s32[]{:S(2)}) async-start(), calls=%async_computation.5 | async-start | bytes 2162688 | tf_op jit(solution)/shard_map/reduce_scatter | solution.py:53
  104.5 58.7 %copy-start.7 = (f32[1,2,64,2048]{3,2,1,0:T(8,128)S(1)}, f32[1,2,64,2048]{3,2,1,0:T(8,128)}, u32[]{:S(2)}) copy-start(f32[1,2,64,2048]{3,2,1,0:T(8,128)} %param.21) | copy-start | bytes 3145732
  163.2 4.3 copy-start.4
  172.0 1.6 copy-start.12
  173.6 401.1 %reduce-scatter.16.cloned.1.call-start = ((), (), s32[]{:S(2)}) async-start(), calls=%async_computation.14 | async-start | bytes 1081344
  338.3 70.6 %collective-permute-start = (f32[128,128]{0,1:T(8,128)S(1)}, f32[128,128]{0,1:T(8,128)S(1)}, u32[]{:S(2)}, u32[]{:S(2)}) collective-permute-start(f32[128,128]{0,1:T(8,128)S(1)} %sub.65), channel_id=1, source_target_pairs={{0,32},{32,0},{64,96},{96,64},{1,33},{33,1},{65,97},{97,65},{2,34}... | collective-permute-start | bytes 196616 | tf_op jit(solution)/shard_map/ppermute | solution.py:10
  417.2 336.1 %reduce-scatter.14.cloned.1.call-start = ((), (), s32[]{:S(2)}) async-start(), calls=%async_computation.6 | async-start | bytes 4325376 | tf_op jit(solution)/shard_map/reduce_scatter | solution.py:53
  574.7 6.1 copy-start.2
  574.7 6.1 copy-start.10
  588.0 165.7 %copy-start.11 = (f32[256,128]{1,0:T(8,128)S(1)}, f32[256,128]{1,0:T(8,128)}, u32[]{:S(2)}) copy-start(f32[256,128]{1,0:T(8,128)} %param.20) | copy-start | bytes 393220
  588.0 204.2 %all-reduce.3.cloned.1.call-start = ((), (), s32[]{:S(2)}) async-start(), calls=%async_computation.7 | async-start | bytes 262144 | tf_op jit(solution)/shard_map/psum | solution.py:66
  753.3 211.5 %reduce-scatter.18.cloned.1.call-start = ((), (), s32[]{:S(2)}) async-start(), calls=%async_computation.15 | async-start | bytes 1081344 | tf_op jit(solution)/shard_map/reduce_scatter | solution.py:53
  803.9 309.5 %all-gather.7.cloned.1.call-start = ((), (), s32[]{:S(2)}) async-start(), calls=%async_computation.8 | async-start | bytes 1081344 | tf_op jit(solution)/shard_map/all_gather | solution.py:49
  964.8 197.4 %all-reduce.5.cloned.1.call-start = ((), (), s32[]{:S(2)}) async-start(), calls=%async_computation.9 | async-start | bytes 262144 | tf_op jit(solution)/shard_map/psum | solution.py:66
  1121.7 199.5 %all-gather.9.cloned.1.call-start = ((), (), s32[]{:S(2)}) async-start(), calls=%async_computation.10 | async-start | bytes 4325376 | tf_op jit(solution)/shard_map/all_gather | solution.py:49
  1162.2 328.1 %all-gather.11.cloned.1.call-start = ((), (), s32[]{:S(2)}) async-start(), calls=%async_computation.11 | async-start | bytes 1081344 | tf_op jit(solution)/shard_map/all_gather | solution.py:49
  1321.1 10.3 copy-start.3
  1321.1 10.4 copy-start.5
  1339.4 285.2 %all-gather.13.cloned.1.call-start = ((), (), s32[]{:S(2)}) async-start(), calls=%async_computation.12 | async-start | bytes 2162688 | tf_op jit(solution)/shard_map/all_gather | solution.py:49
  1497.0 1.3 collective-permute-start.1
  1499.0 299.6 %reduce-scatter.20.cloned.1.call-start = ((), (), s32[]{:S(2)}) async-start(), calls=%async_computation.16 | async-start | bytes 1081344
  1624.6 5.8 copy-start.6
  1635.2 165.0 %copy-start.1 = (s32[2,64]{1,0:T(2,128)S(1)}, s32[2,64]{1,0:T(2,128)}, u32[]{:S(2)}) copy-start(s32[2,64]{1,0:T(2,128)} %param.27) | copy-start | bytes 1540
  1636.3 1.6 copy-start.9
  1636.3 2.3 copy-start.8
Sparse Core Ops, SparseCore 0:
  9.7 153.5 all-gather.14
  173.7 163.6 reduce-scatter.11
  417.3 157.3 reduce-scatter.15
  588.2 165.0 reduce-scatter.13
  755.6 36.6 all-reduce.2
  804.0 160.7 reduce-scatter.17
  966.4 146.9 all-gather.6
  1121.8 40.3 all-reduce.4
  1163.9 157.1 all-gather.8
  1339.5 150.7 all-gather.10
  1499.1 125.4 all-gather.12
  1638.0 160.5 reduce-scatter.19
where the time goes:
time: 1820 us; the launch traced here: 1810 us
  waiting for transfers between devices  1440 us (79%)
  other arithmetic  140 us (8%)
  local copies, waits for them, and re-layouts  133 us (7%)
  matrix products  74.3 us (4%)
    all_gather x5, waiting for transfers between devices, gather_rows(): lax.all_gather(local_rows, 'front', axis=0, tiled=True)  638 us
    reduce_scatter x3, waiting for transfers between devices, scatter_rows(): lax.psum_scatter(term(jnp.int32(0), rows_each * lax.axis_size('front')),...  445 us
    unnamed x14, waiting for transfers between devices  280 us
    gather x2, local copies, waits for them, and re-layouts, pick_rows(): return jnp.take(matrix, sources, axis=1)  90.1 us
    psum x2, waiting for transfers between devices, group_total(): return lax.psum(values, 'leaf')  78.9 us
    and x2, other arithmetic, pick_rows(): return jnp.take(matrix, sources, axis=1)  59.5 us
    select_n x2, other arithmetic, pick_rows(): return jnp.take(matrix, sources, axis=1)  45.9 us
  transfers between devices with their start and end apart: 14, of which 13 were waited for; matrix products, arithmetic and copies ran while one was open for 14% of the time, Pallas kernels for 0%

commit v1 on v0

--- a/solution.py
+++ b/solution.py
@@ -46,7 +46,13 @@
 
 
 def gather_rows(local_rows, update, initial):
-    return update(initial, lax.all_gather(local_rows, "front", axis=0, tiled=True), jnp.int32(0))
+    return update(
+        initial,
+        jnp.concatenate(
+            lax.all_to_all(jnp.stack([local_rows] * lax.axis_size("front")), "front", 0, 0), axis=0
+        ),
+        jnp.int32(0),
+    )
 
 
 def scatter_rows(term, rows_each):

time: 1820 us -> 1300 us (0.71)
  waiting for transfers between devices: 1440 us -> 802 us
  blocking collectives: 0 us -> 128 us
    all_gather x5 -> x0, waiting for transfers between devices: 638 us -> none  [gather_rows(): lax.all_gather(local_rows, 'front', axis=0, tiled=True)]
    all_to_all x0 -> x4, blocking collectives: none -> 128 us  [gather_rows(): lax.all_to_all(jnp.stack([local_rows] * lax.axis_size('front')), 'front',...]
    unnamed x14 -> x9, waiting for transfers between devices: 280 us -> 278 us
  transfers between devices with their start and end apart: 14 -> 10, of which waited for: 13 -> 8; matrix products, arithmetic and copies ran while one was open for 14% -> 20% of each run, Pallas kernels for 0% -> 0%
where the time goes in v1:
time: 1300 us; the launch traced here: 1290 us
  waiting for transfers between devices  802 us (62%)
  other arithmetic  137 us (11%)
  local copies, waits for them, and re-layouts  134 us (10%)
  blocking collectives  128 us (10%)
  matrix products  63.6 us (5%)
  between operations  15.1 us (1%)
    reduce_scatter x3, waiting for transfers between devices, scatter_rows(): lax.psum_scatter(term(jnp.int32(0), rows_each * lax.axis_size('front')),...  447 us
    unnamed x9, waiting for transfers between devices  278 us
    all_to_all x4, blocking collectives, gather_rows(): lax.all_to_all(jnp.stack([local_rows] * lax.axis_size('front')), 'front',...  128 us
    gather x2, local copies, waits for them, and re-layouts, pick_rows(): return jnp.take(matrix, sources, axis=1)  90.6 us
    psum x2, waiting for transfers between devices, group_total(): return lax.psum(values, 'leaf')  75.6 us
    and x2, other arithmetic, pick_rows(): return jnp.take(matrix, sources, axis=1)  59.9 us
    select_n x2, other arithmetic, pick_rows(): return jnp.take(matrix, sources, axis=1)  45.9 us
  transfers between devices with their start and end apart: 10, of which 8 were waited for; matrix products, arithmetic and copies ran while one was open for 20% of the time, Pallas kernels for 0%

profile of v1, /device:TPU:0, one launch (start us, length us, event | category | flops | bytes accessed | tf_op | source)
XLA Modules:
  0.0 1290.3 jit_solution(12815596713042956888)
XLA Ops:
  7.2 2.1 stack.10
  9.3 9.3 all-to-all-start
  18.6 2.3 sort.34
  22.3 20.0 %broadcast_clamp_fusion.1 = s32[4096]{0:T(1024)S(1)} fusion(s32[]{:T(128)} %bitcast.36, s32[]{:T(128)} %bitcast.35, s32[]{:T(128)} %bitcast.34, s32[]{:T(128)} %bitcast.33, s32[]{:T(128)} %bitcast.32, s32[]{:T(128)} %bitcast.31, s32[]{:T(128)} %bitcast.30, s32[]{:T(128)} %bitcast.29, s32[]{:T(128)} %bitcast.28, s32[]{:T(128)} %bitcast.27, s32[]{:T(128)} %bitcast.26, ...), kind=kLoop, calls=%fused_computation.209 | loop fusion | flops 356352 | bytes 16512 | tf_op gather
  42.3 20.0 %compare_and_fusion.1 = pred[4096]{0:T(1024)(128)(4,1)S(1)} fusion(s32[]{:T(128)} %bitcast.36, s32[]{:T(128)} %bitcast.35, s32[]{:T(128)} %bitcast.34, s32[]{:T(128)} %bitcast.33, s32[]{:T(128)} %bitcast.32, s32[]{:T(128)} %bitcast.31, s32[]{:T(128)} %bitcast.30, s32[]{:T(128)} %bitcast.29, s32[]{:T(128)} %bitcast.28, s32[]{:T(128)} %bitcast.27, ...), kind=kLoop, calls=%fused_computation.208 | loop fusion | flops 364544 | bytes 4224 | tf_op jit(solution)/shard_map/jit(_take)/and | solution.py:45
  62.3 4.4 copy.40
  66.7 30.8 %gather_fusion = f32[4096,2,64]{2,1,0:T(2,128)} fusion(f32[2,4096,64]{2,0,1:T(2,128)} %bitcast.210, s32[4096]{0:T(1024)S(1)} %broadcast_clamp_fusion.1), kind=kCustom, calls=%fused_computation.clone | custom fusion | bytes 4210688 | tf_op jit(solution)/shard_map/jit(_take)/gather | solution.py:45
  97.5 16.3 %select_bitcast_fusion.1 = f32[2,4096,64]{2,0,1:T(2,128)S(1)} fusion(f32[4096,2,64]{2,1,0:T(2,128)} %gather_fusion, pred[4096]{0:T(1024)(128)(4,1)S(1)} %compare_and_fusion.1), kind=kLoop, calls=%fused_computation.4 | loop fusion | flops 524288 | bytes 4198400 | tf_op jit(solution)/shard_map/jit(_take)/select_n | solution.py:45
  113.8 4.1 fusion.156
  117.9 1.9 fusion.25
  119.9 1.8 fusion.28
  121.9 2.1 fusion.163
  124.0 2.1 fusion.164
  126.4 1.5 pad_maximum_fusion.1
  128.1 2.0 sort.35
  133.4 39.9 %compare_and_fusion = (pred[8192]{0:T(1024)(128)(4,1)S(1)}, s32[8192]{0:T(1024)S(1)}) fusion(s32[]{:T(128)} %bitcast.110, s32[]{:T(128)} %bitcast.109, s32[]{:T(128)} %bitcast.108, s32[]{:T(128)} %bitcast.107, s32[]{:T(128)} %bitcast.106, s32[]{:T(128)} %bitcast.105, s32[]{:T(128)} %bitcast.104, s32[]{:T(128)} %bitcast.103, s32[]{:T(128)} %bitcast.102, ...), kind=kLoop, calls=%fused_computation.164 | loop fusion | flops 1253376 | bytes 41216 | tf_op jit(solution)/shard_map/jit(_take)/and | solution.py:45
  173.3 119.5 %reduce-scatter.12.cloned.1.call-done = f32[128,128]{0,1:T(8,128)} async-done(((f32[4096,128]{0,1:T(8,128)}), f32[128,128]{0,1:T(8,128)}) %reduce-scatter.12.cloned.1.call-update) | async-done | bytes 65552 | tf_op jit(solution)/shard_map/reduce_scatter | solution.py:59
  293.9 10.8 copy.42
  304.7 59.9 %gather_fusion.1 = f32[8192,2,64]{2,1,0:T(2,128)} fusion(f32[2,8192,64]{2,0,1:T(2,128)} %bitcast.203, s32[8192]{0:T(1024)S(1)} %broadcast_clamp_fusion), kind=kCustom, calls=%fused_computation.1.clone | custom fusion | bytes 8421376 | tf_op jit(solution)/shard_map/jit(_take)/gather | solution.py:45
  364.6 2.2 convolution_bitcast_fusion.3
  366.8 2.2 convolution_bitcast_fusion.2
  369.3 1.4 copy.51
  370.8 29.5 %select_bitcast_fusion = f32[2,8192,64]{2,0,1:T(2,128)S(1)} fusion(f32[8192,2,64]{2,1,0:T(2,128)} %gather_fusion.1, pred[8192]{0:T(1024)(128)(4,1)S(1)} %get-tuple-element.20), kind=kLoop, calls=%fused_computation.2 | loop fusion | flops 1048576 | bytes 8396800 | tf_op jit(solution)/shard_map/jit(_take)/select_n | solution.py:45
  400.3 7.7 fusion.155
  408.1 120.1 %reduce-scatter.16.cloned.1.call-done = f32[64,128]{1,0:T(8,128)} async-done(((f32[2048,128]{1,0:T(8,128)}), f32[64,128]{1,0:T(8,128)}) %reduce-scatter.16.cloned.1.call-update) | async-done | bytes 32784
  528.2 6.0 fusion.165
  534.3 4.4 fusion.166
  539.2 2.3 pad_maximum_fusion
  541.6 165.4 %reduce-scatter.14.cloned.1.call-done = f32[256,128]{0,1:T(8,128)} async-done(((f32[8192,128]{0,1:T(8,128)}), f32[256,128]{0,1:T(8,128)}) %reduce-scatter.14.cloned.1.call-update) | async-done | bytes 131088 | tf_op jit(solution)/shard_map/reduce_scatter | solution.py:59
  707.5 37.7 %all-reduce.3.cloned.1.call-done = f32[256,128]{0,1:T(8,128)} async-done(((f32[256,128]{0,1:T(8,128)}), f32[256,128]{0,1:T(8,128)}) %all-reduce.3.cloned.1.call-update) | async-done | bytes 131088 | tf_op jit(solution)/shard_map/psum | solution.py:72
  745.3 3.9 convolution_bitcast_fusion.5
  749.1 3.9 convolution_bitcast_fusion.4
  753.3 1.4 copy.53
  754.8 162.3 %reduce-scatter.18.cloned.1.call-done = f32[64,128]{1,0:T(8,128)} async-done(((f32[2048,128]{1,0:T(8,128)}), f32[64,128]{1,0:T(8,128)}) %reduce-scatter.18.cloned.1.call-update) | async-done | bytes 32784 | tf_op jit(solution)/shard_map/reduce_scatter | solution.py:59
  918.1 16.1 %all_to_all.25 = f32[32,64,128]{2,1,0:T(8,128)S(1)} all-to-all(f32[32,64,128]{2,1,0:T(8,128)S(1)} %stack.11), channel_id=1, replica_groups=mesh['leaf'=4,'front'=32] {'front'}, dimensions={0} | all-to-all | bytes 2097152 | tf_op jit(solution)/shard_map/all_to_all | solution.py:52
  934.2 3.4 fusion.10
  937.6 1.9 fusion.13
  940.3 37.8 %all-reduce.5.cloned.1.call-done = f32[256,128]{0,1:T(8,128)} async-done(((f32[256,128]{0,1:T(8,128)}), f32[256,128]{0,1:T(8,128)}) %all-reduce.5.cloned.1.call-update) | async-done | bytes 131088 | tf_op jit(solution)/shard_map/psum | solution.py:72
  979.6 58.4 %all_to_all.26 = f32[32,256,128]{2,1,0:T(8,128)S(1)} all-to-all(f32[32,256,128]{2,1,0:T(8,128)S(1)} %stack.12), channel_id=1, replica_groups=mesh['leaf'=4,'front'=32] {'front'}, dimensions={0} | all-to-all | bytes 8388608 | tf_op jit(solution)/shard_map/all_to_all | solution.py:52
  1038.0 7.1 fusion.167
  1045.2 7.3 fusion.168
  1052.8 20.6 %all_to_all.27 = f32[32,64,128]{2,1,0:T(8,128)S(1)} all-to-all(f32[32,64,128]{2,1,0:T(8,128)S(1)} %stack.13), channel_id=1, replica_groups=mesh['leaf'=4,'front'=32] {'front'}, dimensions={0} | all-to-all | bytes 2097152 | tf_op jit(solution)/shard_map/all_to_all | solution.py:52
  1073.5 1.9 convolution_bitcast_fusion.6
  1075.3 1.9 convolution_bitcast_fusion.7
  1078.9 32.7 %all_to_all.28 = f32[32,128,128]{2,1,0:T(8,128)S(1)} all-to-all(f32[32,128,128]{2,1,0:T(8,128)S(1)} %stack.14), channel_id=1, replica_groups=mesh['leaf'=4,'front'=32] {'front'}, dimensions={0} | all-to-all | bytes 4194304 | tf_op jit(solution)/shard_map/all_to_all | solution.py:52
  1111.6 3.6 fusion.169
  1115.1 3.7 fusion.170
  1123.5 158.1 %reduce-scatter.20.cloned.1.call-done = f32[64,128]{1,0:T(8,128)} async-done(((f32[2048,128]{1,0:T(8,128)}), f32[64,128]{1,0:T(8,128)}) %reduce-scatter.20.cloned.1.call-update) | async-done | bytes 32784
  (95 shorter events, 19.4 us)
Async XLA Ops:
  7.2 120.9 %copy-start = (s32[2,64]{1,0:T(2,128)S(1)}, s32[2,64]{1,0:T(2,128)}, u32[]{:S(2)}) copy-start(s32[2,64]{1,0:T(2,128)} %param.27) | copy-start | bytes 1540
  7.2 55.1 %copy-start.10 = (f32[1,2,4096,64]{2,3,1,0:T(8,128)S(1)}, f32[1,2,4096,64]{2,3,1,0:T(8,128)}, u32[]{:S(2)}) copy-start(f32[1,2,4096,64]{2,3,1,0:T(8,128)} %param.22) | copy-start | bytes 6291460
  9.3 108.7 %all-to-all-start = ((f32[32,64,128]{2,1,0:T(8,128)}), f32[32,64,128]{2,1,0:T(8,128)S(1)}, u32[]{:S(2)}, u32[]{:S(2)}) async-start(f32[32,64,128]{2,1,0:T(8,128)} %stack.10), calls=%async_computation | async-start | bytes 2097152 | tf_op jit(solution)/shard_map/all_to_all | solution.py:52
  18.5 274.3 %reduce-scatter.12.cloned.1.call-start = ((), (), s32[]{:S(2)}) async-start(), calls=%async_computation.10 | async-start | bytes 2162688 | tf_op jit(solution)/shard_map/reduce_scatter | solution.py:59
  117.9 3.9 copy-start.5
  126.4 1.6 copy-start.14
  127.9 400.3 %reduce-scatter.16.cloned.1.call-start = ((), (), s32[]{:S(2)}) async-start(), calls=%async_computation.14 | async-start | bytes 1081344
  293.7 70.9 %collective-permute-start = (f32[128,128]{0,1:T(8,128)S(1)}, f32[128,128]{0,1:T(8,128)S(1)}, u32[]{:S(2)}, u32[]{:S(2)}) collective-permute-start(f32[128,128]{0,1:T(8,128)S(1)} %sub.65), channel_id=1, source_target_pairs={{0,32},{32,0},{64,96},{96,64},{1,33},{33,1},{65,97},{97,65},{2,34}... | collective-permute-start | bytes 196616 | tf_op jit(solution)/shard_map/ppermute | solution.py:10
  370.7 336.2 %reduce-scatter.14.cloned.1.call-start = ((), (), s32[]{:S(2)}) async-start(), calls=%async_computation.11 | async-start | bytes 4325376 | tf_op jit(solution)/shard_map/reduce_scatter | solution.py:59
  528.2 6.1 copy-start.2
  528.2 6.1 copy-start.12
  541.5 165.9 %copy-start.13 = (f32[256,128]{1,0:T(8,128)S(1)}, f32[256,128]{1,0:T(8,128)}, u32[]{:S(2)}) copy-start(f32[256,128]{1,0:T(8,128)} %param.20) | copy-start | bytes 393220
  541.5 203.7 %all-reduce.3.cloned.1.call-start = ((), (), s32[]{:S(2)}) async-start(), calls=%async_computation.12 | async-start | bytes 262144 | tf_op jit(solution)/shard_map/psum | solution.py:72
  706.9 210.1 %reduce-scatter.18.cloned.1.call-start = ((), (), s32[]{:S(2)}) async-start(), calls=%async_computation.15 | async-start | bytes 1081344 | tf_op jit(solution)/shard_map/reduce_scatter | solution.py:59
  754.7 223.4 %all-reduce.5.cloned.1.call-start = ((), (), s32[]{:S(2)}) async-start(), calls=%async_computation.13 | async-start | bytes 262144 | tf_op jit(solution)/shard_map/psum | solution.py:72
  917.1 20.5 %copy-start.7 = (f32[2,2048,256]{2,1,0:T(8,128)S(1)}, f32[2,2048,256]{2,1,0:T(8,128)}, u32[]{:S(2)}) copy-start(f32[2,2048,256]{2,1,0:T(8,128)} %param.25) | copy-start | bytes 12582916
  940.2 341.3 %reduce-scatter.20.cloned.1.call-start = ((), (), s32[]{:S(2)}) async-start(), calls=%async_computation.16 | async-start | bytes 1081344
  979.1 58.9 %copy-start.11 = (f32[256,128]{1,0:T(8,128)}, f32[256,128]{1,0:T(8,128)S(1)}, u32[]{:S(2)}) copy-start(f32[256,128]{1,0:T(8,128)S(1)} %copy.45) | copy-start | bytes 393220
  979.6 58.4 %copy-start.4 = (f32[1,8192,64]{2,0,1:T(1,128)S(1)}, f32[1,8192,64]{2,0,1:T(1,128)}, u32[]{:S(2)}) copy-start(f32[1,8192,64]{2,0,1:T(1,128)} %get-tuple-element.24) | copy-start | bytes 6291460
  1038.0 7.1 copy-start.3
  1045.2 28.3 %copy-start.8 = (f32[1,2,2048,128]{3,2,1,0:T(8,128)S(1)}, f32[1,2,2048,128]{3,2,1,0:T(8,128)}, u32[]{:S(2)}) copy-start(f32[1,2,2048,128]{3,2,1,0:T(8,128)} %param.23) | copy-start | bytes 6291460
  1077.2 1.3 collective-permute-start.1
  1078.7 32.9 %copy-start.6 = (f32[1,4096,64]{2,0,1:T(1,128)S(1)}, f32[1,4096,64]{2,0,1:T(1,128)}, u32[]{:S(2)}) copy-start(f32[1,4096,64]{2,0,1:T(1,128)} %get-tuple-element.28) | copy-start | bytes 3145732
  1111.6 7.3 copy-start.9
  1120.0 163.1 %copy-start.1 = (s32[2,64]{1,0:T(2,128)S(1)}, s32[2,64]{1,0:T(2,128)}, u32[]{:S(2)}) copy-start(s32[2,64]{1,0:T(2,128)} %param.27) | copy-start | bytes 1540
Sparse Core Ops, SparseCore 0:
  128.0 164.7 reduce-scatter.11
  370.8 157.3 reduce-scatter.15
  541.6 165.2 reduce-scatter.13
  709.2 35.9 all-reduce.2
  754.8 162.2 reduce-scatter.17
  940.3 37.7 all-reduce.4
  1122.8 158.6 reduce-scatter.19
